TPU v7x, 32 devices: a whole 2x2x4 slice. The times are simulated.
32 devices in a mesh: slab: 2 (over y), ang: 4 (over z), row: 2 (over x), ch: 2 (over core).
Axes of the slice: x: 2, y: 2, z: 4, core: 2. Of those that a mesh axis runs over, the one named last changes fastest.
Arguments:
- projections: float32 [8, 64, 2048], P(('slab', 'ang'), 'row'), parts along dimension 0, may hold values from -6 to 6
- conv1_weight: float32 [8, 3, 3], P('ch'), may hold values from -2 to 2
- conv1_bias: float32 [8], P('ch'), may hold values from -0.5 to 0.5
- filter_taps: float32 [8, 2048], P('ch'), may hold values from -0.125 to 0.125
- conv2_weight: float32 [8, 3, 3], replicated, may hold values from -0.75 to 0.75
- cotangent: float32 [4, 4, 32, 2048], P(('slab', 'row'), None, ('ang', 'ch')), parts along dimension 0, may hold values from -0.0029296875 to 0.0029296875
Outputs:
- sinogram: float32 [4, 4, 32, 2048], P(('slab', 'row'), None, ('ang', 'ch')), parts along dimension 0
- grad_conv1: float32 [16, 3, 3], P(('slab', 'ch')), parts along dimension 0
- grad_bias: float32 [16], P(('slab', 'ch')), parts along dimension 0
- grad_taps: float32 [16, 2048], P(('slab', 'ch')), parts along dimension 0
- grad_conv2: float32 [16, 3, 3], P(('slab', 'ch')), parts along dimension 0
There are 2 independent parts, one for each index of `slab`. A program takes and returns all parts, laid end to end along the dimension named above; an argument that names none is the same for every part. Nothing has to cross between parts.
All inputs are finite; a program needn't handle non-finite values.
Results may differ from a plain program's by a relative error of at most 0.00028.
Values sent between devices are 32-bit elements; how exact they have to be, the bound alone decides.
A program may use at most 64 MiB of HBM per device.

v0:
```python
import functools
import math

import jax
import jax.numpy as jnp
import numpy as np
import ml_dtypes
from jax import lax
from jax.experimental import pallas as pl
from jax.experimental.pallas import tpu as pltpu
from jax.sharding import PartitionSpec as P

MESH = pl.DeviceIdType.MESH
LANES = 128
SLOTS = 32


def twisted(value, k, n, sign):
    re, im = value
    if k == 0:
        return value
    if 4 * k == n:
        return (-im, re) if sign > 0 else (im, -re)
    if 8 * k == n:
        half = math.sqrt(0.5)
        return (half * (re - sign * im), half * (im + sign * re))
    if 8 * k == 3 * n:
        half = math.sqrt(0.5)
        return (half * (-re - sign * im), half * (-im + sign * re))
    cos = math.cos(2 * math.pi * k / n)
    sin = sign * math.sin(2 * math.pi * k / n)
    return (cos * re - sin * im, cos * im + sin * re)


def short_dft(values, sign):
    n = len(values)
    if n == 1:
        return values
    even = short_dft(values[0::2], sign)
    odd = short_dft(values[1::2], sign)
    low, high = [], []
    for k in range(n // 2):
        re, im = twisted(odd[k], k, n, sign)
        low.append((even[k][0] + re, even[k][1] + im))
        high.append((even[k][0] - re, even[k][1] - im))
    return low + high


def split_high_low(table):
    high = table.astype(ml_dtypes.bfloat16)
    low = (table - high.astype(np.float64)).astype(ml_dtypes.bfloat16)
    return high, low


def make_tables(length):
    outer = length // LANES
    index = np.arange(LANES)
    inner = 2 * np.pi * (np.outer(index, index) % LANES) / LANES
    cos, sin = np.cos(inner), np.sin(inner)
    forward = np.block([[cos, -sin], [sin, cos]])
    inverse = np.block([[cos, sin], [-sin, cos]]) / length
    twist = 2 * np.pi * np.outer(np.arange(outer), index) / length
    twist = np.repeat(twist, 8, axis=0)
    tables = np.stack([*split_high_low(forward), *split_high_low(inverse)])
    turns = np.stack([np.cos(twist), np.sin(twist)]).astype(np.float32)
    return tables, turns


def multiply(ref, start, rows, tables_ref, which):
    values = ref[pl.ds(start, rows), :]
    high = values.astype(jnp.bfloat16)
    low = (values - high.astype(jnp.float32)).astype(jnp.bfloat16)
    dot = functools.partial(jnp.dot, preferred_element_type=jnp.float32)
    table_high = tables_ref[which]
    ref[pl.ds(start, rows), :] = (
        dot(high, table_high) + dot(low, table_high) + dot(high, tables_ref[which + 1])
    )


def kernel(
    sizes,
    rows_ref, packed_ref, taps_ref, second_ref, cot_ref, tables_ref, turns_ref,
    sino_ref, taps_out_ref, small_out_ref,
    got, top, bottom, all_taps, all_packed, first_ref,
    cot_shift, proj_shift, spec_back, spec_hidden, spec_taps, work,
    back, slope, filt, partial, mixed,
    outgoing, incoming, collected,
    rows_send, rows_recv, edge_send, edge_recv, taps_send, taps_recv,
    packed_send, packed_recv, sum_send, sum_recv, gather_send, gather_recv, local_sem,
):
    ang_n, row_n, ch_n = sizes
    n = ang_n * row_n * ch_n
    angles, rq, columns = cot_ref.shape
    chans = second_ref.shape[0]
    chans_dev = taps_ref.shape[0]
    held = rows_ref.shape[0] - 2
    both = angles * rq
    half = both // 2
    outer = columns // LANES
    block = outer * half
    slab = lax.axis_index("slab")
    z, k, c0 = lax.axis_index("ang"), lax.axis_index("row"), lax.axis_index("ch")
    me = (z * row_n + k) * ch_n + c0

    def place(d):
        return (slab, d // (row_n * ch_n), d // ch_n % row_n, d % ch_n)

    barrier = pltpu.get_barrier_semaphore()

    @pl.loop(1, n)
    def _(o):
        pl.semaphore_signal(barrier, inc=1, device_id=place((me + o) % n), device_id_type=MESH)

    pl.semaphore_wait(barrier, n - 1)

    def rows_copy(o, slot, target):
        start = (target * ch_n + c0) * rq
        return pltpu.make_async_remote_copy(
            src_ref=rows_ref.at[pl.ds(start, rq + 2)], dst_ref=got.at[slot],
            send_sem=rows_send.at[o], recv_sem=rows_recv.at[slot],
            device_id=(slab, target, k, c0), device_id_type=MESH)

    def taps_copy(o, slot, target):
        return pltpu.make_async_remote_copy(
            src_ref=taps_ref, dst_ref=all_taps.at[slot],
            send_sem=taps_send.at[o], recv_sem=taps_recv.at[slot],
            device_id=(slab, z, k, target), device_id_type=MESH)

    def packed_copy(o, slot, target):
        return pltpu.make_async_remote_copy(
            src_ref=packed_ref, dst_ref=all_packed.at[slot],
            send_sem=packed_send.at[o], recv_sem=packed_recv.at[slot],
            device_id=(slab, z, k, target), device_id_type=MESH)

    def top_copy(slot):
        return pltpu.make_async_remote_copy(
            src_ref=rows_ref.at[held], dst_ref=top.at[slot],
            send_sem=edge_send.at[0], recv_sem=edge_recv.at[0, slot],
            device_id=(slab, 0, (k + 1) % row_n, 0), device_id_type=MESH)

    def bottom_copy(slot):
        return pltpu.make_async_remote_copy(
            src_ref=rows_ref.at[1], dst_ref=bottom.at[slot],
            send_sem=edge_send.at[1], recv_sem=edge_recv.at[1, slot],
            device_id=(slab, ang_n - 1, (k + row_n - 1) % row_n, ch_n - 1), device_id_type=MESH)

    for o in range(1, ch_n):
        taps_copy(o, c0, (c0 + o) % ch_n).start()
        packed_copy(o, c0, (c0 + o) % ch_n).start()
    sends_top = jnp.logical_and(c0 == 0, k < row_n - 1)
    sends_bottom = jnp.logical_and(c0 == ch_n - 1, k > 0)

    @pl.when(sends_top)
    def _():
        top_copy(z).start()

    @pl.when(sends_bottom)
    def _():
        bottom_copy(z).start()

    for o in range(1, ang_n):
        rows_copy(o, z, (z + o) % ang_n).start()

    got[z] = rows_ref[pl.ds((z * ch_n + c0) * rq, rq + 2)]
    all_taps[c0] = taps_ref[...]
    all_packed[c0] = packed_ref[...]

    column = lax.broadcasted_iota(jnp.int32, (both, columns), 1)
    first_col, last_col = column == 0, column == columns - 1

    def from_left(x):
        return jnp.where(first_col, 0.0, pltpu.roll(x, 1, 1))

    def from_right(x):
        return jnp.where(last_col, 0.0, pltpu.roll(x, columns - 1, 1))

    def cols(m):
        return slice(m * LANES, (m + 1) * LANES)

    lo, hi = slice(0, half), slice(half, both)
    re_l, im_l = slice(0, LANES), slice(LANES, 2 * LANES)

    upstream = jnp.concatenate([cot_ref[a] for a in range(angles)], axis=0)
    for i in range(3):
        shift = (i - 1) * rq % both
        turned = pltpu.roll(upstream, shift, 0) if shift else upstream
        cot_shift[3 * i] = from_right(turned)
        cot_shift[3 * i + 1] = turned
        cot_shift[3 * i + 2] = from_left(turned)

    def store_forward(ref, start, values):
        for q, (re, im) in enumerate(short_dft(values, -1)):
            part = slice(q * half, (q + 1) * half)
            cos, sin = turns_ref[0, part, :], turns_ref[1, part, :]
            rows = pl.ds(start + q * half, half)
            ref[rows, re_l] = re * cos + im * sin
            ref[rows, im_l] = im * cos - re * sin

    def load_inverse(ref, start):
        values = []
        for q in range(outer):
            part = slice(q * half, (q + 1) * half)
            cos, sin = turns_ref[0, part, :], turns_ref[1, part, :]
            rows = pl.ds(start + q * half, half)
            re, im = ref[rows, re_l], ref[rows, im_l]
            values.append((re * cos - im * sin, im * cos + re * sin))
        return short_dft(values, 1)

    def start_of(c):
        return pl.multiple_of(c * block, block)

    @pl.loop(0, chans)
    def _(c):
        weights = [second_ref[c, t // 3, t % 3] for t in range(9)]
        values = []
        for m in range(outer):
            pair = []
            for rows in (lo, hi):
                total = weights[0] * cot_shift[0, rows, cols(m)]
                for t in range(1, 9):
                    total = total + weights[t] * cot_shift[t, rows, cols(m)]
                pair.append(total)
            values.append(tuple(pair))
        store_forward(spec_back, start_of(c), values)

    step = 4 * block
    for s in range(0, chans * block, step):
        multiply(spec_back, s, step, tables_ref, 0)

    for o in range(1, ch_n):
        source = (c0 + o) % ch_n
        taps_copy(o, source, source).wait_recv()
        packed_copy(o, source, source).wait_recv()
    load_weights = pltpu.make_async_copy(all_packed, first_ref, local_sem)
    load_weights.start()
    taps = jnp.concatenate([all_taps[h] for h in range(ch_n)], axis=0)
    zero = jnp.zeros((chans, LANES), jnp.float32)
    store_forward(spec_taps, 0, [(taps[:, cols(m)], zero) for m in range(outer)])
    multiply(spec_taps, 0, block, tables_ref, 0)

    def tap_row(q, c):
        row = spec_taps[pl.ds(q * half + c, 1), :]
        row = jnp.broadcast_to(row, (half, 2 * LANES))
        return row[:, re_l], row[:, im_l]

    @pl.loop(0, chans)
    def _(c):
        for q in range(outer):
            tr, ti = tap_row(q, c)
            rows = pl.ds(start_of(c) + q * half, half)
            gr, gi = spec_back[rows, re_l], spec_back[rows, im_l]
            work[rows, re_l] = tr * gr - ti * gi
            work[rows, im_l] = tr * gi + ti * gr

    for s in range(0, chans * block, step):
        multiply(work, s, step, tables_ref, 2)

    @pl.loop(0, chans)
    def _(c):
        for m, (re, im) in enumerate(load_inverse(work, start_of(c))):
            back[c, lo, cols(m)] = re
            back[c, hi, cols(m)] = im

    load_weights.wait()
    for o in range(1, ang_n):
        source = (z + o) % ang_n
        rows_copy(o, source, source).wait_recv()

    @pl.when(jnp.logical_and(jnp.logical_and(z == 0, c0 == 0), k > 0))
    def _():
        for a in range(ang_n):
            top_copy(a).wait_recv()
            got[a, 0] = top[a]

    @pl.when(jnp.logical_and(jnp.logical_and(z == ang_n - 1, c0 == ch_n - 1), k < row_n - 1))
    def _():
        for a in range(ang_n):
            bottom_copy(a).wait_recv()
            got[a, rq + 1] = bottom[a]

    for a in range(angles):
        for r in range(rq + 2):
            line = got[a, r]
            for i in range(3):
                q = r - i
                if 0 <= q < rq:
                    for m in range(outer):
                        proj_shift[3 * i + 1, a * rq + q : a * rq + q + 1, cols(m)] = line[m : m + 1, :]
    for i in range(3):
        centre = proj_shift[3 * i + 1]
        proj_shift[3 * i] = from_left(centre)
        proj_shift[3 * i + 2] = from_right(centre)

    @pl.loop(0, chans)
    def _(c):
        h, l = c // chans_dev, c % chans_dev
        weights = [first_ref[h, l, t] for t in range(10)]
        values = []
        for m in range(outer):
            pair = []
            for rows in (lo, hi):
                pre = weights[9] + weights[0] * proj_shift[0, rows, cols(m)]
                for t in range(1, 9):
                    pre = pre + weights[t] * proj_shift[t, rows, cols(m)]
                gate = 0.5 + 0.5 * jnp.tanh(0.5 * pre)
                slope[c, rows, cols(m)] = gate * (1.0 + pre * (1.0 - gate))
                pair.append(pre * gate)
            values.append(tuple(pair))
        store_forward(spec_hidden, start_of(c), values)

    for s in range(0, chans * block, step):
        multiply(spec_hidden, s, step, tables_ref, 0)
    work[pl.ds(chans * block, block), :] = jnp.zeros((block, 2 * LANES), jnp.float32)
    line_of = lax.broadcasted_iota(jnp.int32, (half, LANES), 0)

    def folded(value):
        return jnp.sum(value, axis=0, keepdims=True)


    @pl.loop(0, chans)
    def _(c):
        for q in range(outer):
            tr, ti = tap_row(q, c)
            rows = pl.ds(start_of(c) + q * half, half)
            gr, gi = spec_back[rows, re_l], spec_back[rows, im_l]
            hr, hi_ = spec_hidden[rows, re_l], spec_hidden[rows, im_l]
            work[rows, re_l] = tr * hr + ti * hi_
            work[rows, im_l] = tr * hi_ - ti * hr
            at = slice(chans * block + q * half, chans * block + (q + 1) * half)
            work[at, re_l] = jnp.where(line_of == c, folded(gr * hr + gi * hi_), work[at, re_l])
            work[at, im_l] = jnp.where(line_of == c, folded(gr * hi_ - gi * hr), work[at, im_l])

    for s in range(0, chans * block, step):
        multiply(work, s, step, tables_ref, 2)
    multiply(work, chans * block, block, tables_ref, 2)
    partial[...] = jnp.zeros(partial.shape, jnp.float32)

    @pl.loop(0, chans)
    def _(c):
        sums = [jnp.zeros((half, LANES), jnp.float32) for _ in range(9)]
        for m, (re, im) in enumerate(load_inverse(work, start_of(c))):
            filt[c, lo, cols(m)] = re
            filt[c, hi, cols(m)] = im
            for t in range(9):
                sums[t] = sums[t] + re * cot_shift[t, lo, cols(m)] + im * cot_shift[t, hi, cols(m)]
        for t in range(9):
            partial[c, 16 + t : 17 + t, :] = folded(sums[t])

    @pl.loop(0, chans)
    def _(c):
        sums = [jnp.zeros((half, LANES), jnp.float32) for _ in range(10)]
        for m in range(outer):
            for rows in (lo, hi):
                grad = back[c, rows, cols(m)] * slope[c, rows, cols(m)]
                for t in range(9):
                    sums[t] = sums[t] + grad * proj_shift[t, rows, cols(m)]
                sums[9] = sums[9] + grad
        for t in range(10):
            partial[c, t : t + 1, :] = folded(sums[t])

    small = lax.dot_general(
        jnp.ones((8, LANES), jnp.float32), partial[...].reshape(chans * SLOTS, LANES), (((1,), (1,)), ((), ())),
        precision=lax.Precision.HIGHEST, preferred_element_type=jnp.float32)
    width = chans_dev * SLOTS
    for m, (re, im) in enumerate(load_inverse(work, chans * block)):
        outgoing[m, 0:chans, :] = re
        h = m % ch_n
        outgoing[m, chans : chans + 1, :] = small[0:1, h * width : (h + 1) * width]

    def sum_copy(o, slot, target):
        return pltpu.make_async_remote_copy(
            src_ref=outgoing.at[target % outer], dst_ref=incoming.at[slot],
            send_sem=sum_send.at[o], recv_sem=sum_recv.at[slot],
            device_id=place(target), device_id_type=MESH)

    @pl.loop(1, n)
    def _(o):
        sum_copy(o, me, (me + o) % n).start()

    incoming[me] = outgoing[me % outer]

    @pl.loop(0, outer)
    def _(m):
        at = pl.ds(pl.multiple_of(m * LANES, LANES), LANES)
        for rows in (lo, hi):
            pieces = [filt[c, rows, at] for c in range(chans)]
            for t in range(9):
                total = second_ref[0, t // 3, t % 3] * pieces[0]
                for c in range(1, chans):
                    total = total + second_ref[c, t // 3, t % 3] * pieces[c]
                mixed[t, rows, at] = total

    sides = []
    for j in range(3):
        total = mixed[3 + j]
        for i in (0, 2):
            total = total + pltpu.roll(mixed[3 * i + j], -(i - 1) * rq % both, 0)
        sides.append(total)
    image = sides[1] + from_left(sides[0]) + from_right(sides[2])
    for a in range(angles):
        sino_ref[a] = image[a * rq : (a + 1) * rq]

    @pl.loop(1, n)
    def _(o):
        source = (me + o) % n
        sum_copy(o, source, source).wait_recv()

    total = incoming[0]
    for d in range(1, n):
        total = total + incoming[d]
    small_out_ref[...] = jnp.broadcast_to(total[chans : chans + 1], small_out_ref.shape)
    mine = me % outer
    group = me - mine
    collected[mine] = total[0:chans]

    def gather_copy(o, slot, target):
        return pltpu.make_async_remote_copy(
            src_ref=collected.at[mine], dst_ref=collected.at[slot],
            send_sem=gather_send.at[o], recv_sem=gather_recv.at[slot],
            device_id=place(group + target), device_id_type=MESH)

    @pl.loop(1, outer)
    def _(o):
        gather_copy(o, mine, (mine + o) % outer).start()

    @pl.loop(1, outer)
    def _(o):
        source = (mine + o) % outer
        gather_copy(o, source, source).wait_recv()

    for m in range(outer):
        taps_out_ref[:, cols(m)] = collected[m, pl.ds(c0 * chans_dev, chans_dev), :]

    for o in range(1, ang_n):
        rows_copy(o, z, (z + o) % ang_n).wait_send()
    for o in range(1, ch_n):
        taps_copy(o, c0, (c0 + o) % ch_n).wait_send()
        packed_copy(o, c0, (c0 + o) % ch_n).wait_send()

    @pl.when(sends_top)
    def _():
        top_copy(z).wait_send()

    @pl.when(sends_bottom)
    def _():
        bottom_copy(z).wait_send()

    @pl.loop(1, n)
    def _(o):
        sum_copy(o, me, (me + o) % n).wait_send()

    @pl.loop(1, outer)
    def _(o):
        gather_copy(o, mine, (mine + o) % outer).wait_send()


def on_device(sizes, tables, projections, conv1_weight, conv1_bias, filter_taps, conv2_weight, cotangent):
    ang_n, row_n, ch_n = sizes
    n = ang_n * row_n * ch_n
    _, held, columns = projections.shape
    chans_dev = conv1_weight.shape[0]
    chans = chans_dev * ch_n
    _, angles, rq, _ = cotangent.shape
    outer = columns // LANES
    both = angles * rq
    block = outer * both // 2
    rows = jnp.pad(projections[0], ((1, 1), (0, 0))).reshape(held + 2, outer, LANES)
    packed = jnp.concatenate([conv1_weight.reshape(chans_dev, 9), conv1_bias[:, None]], axis=1)
    packed = jnp.pad(packed, ((0, 0), (0, LANES - 10)))
    f32 = jnp.float32
    vmem = pl.BlockSpec(memory_space=pltpu.VMEM)
    dma = pltpu.SemaphoreType.DMA
    wide = (both, columns)
    image, taps_out, small = pl.pallas_call(
        functools.partial(kernel, sizes),
        out_shape=(
            jax.ShapeDtypeStruct((angles, rq, columns), f32),
            jax.ShapeDtypeStruct((chans_dev, columns), f32),
            jax.ShapeDtypeStruct((8, LANES), f32),
        ),
        in_specs=[vmem, vmem, vmem, pl.BlockSpec(memory_space=pltpu.SMEM), vmem, vmem, vmem],
        out_specs=(vmem, vmem, vmem),
        scratch_shapes=[
            pltpu.VMEM((ang_n, rq + 2, outer, LANES), f32),
            pltpu.VMEM((ang_n, outer, LANES), f32),
            pltpu.VMEM((ang_n, outer, LANES), f32),
            pltpu.VMEM((ch_n, chans_dev, columns), f32),
            pltpu.VMEM((ch_n, chans_dev, LANES), f32),
            pltpu.SMEM((ch_n, chans_dev, LANES), f32),
            pltpu.VMEM((9,) + wide, f32),
            pltpu.VMEM((9,) + wide, f32),
            pltpu.VMEM((chans * block, 2 * LANES), f32),
            pltpu.VMEM((chans * block, 2 * LANES), f32),
            pltpu.VMEM((block, 2 * LANES), f32),
            pltpu.VMEM(((chans + 1) * block, 2 * LANES), f32),
            pltpu.VMEM((chans,) + wide, f32),
            pltpu.VMEM((chans,) + wide, f32),
            pltpu.VMEM((chans,) + wide, f32),
            pltpu.VMEM((chans, SLOTS, LANES), f32),
            pltpu.VMEM((9,) + wide, f32),
            pltpu.VMEM((outer, chans + 1, LANES), f32),
            pltpu.VMEM((n, chans + 1, LANES), f32),
            pltpu.VMEM((outer, chans, LANES), f32),
            dma((ang_n,)), dma((ang_n,)), dma((2,)), dma((2, ang_n)),
            dma((ch_n,)), dma((ch_n,)), dma((ch_n,)), dma((ch_n,)),
            dma((n,)), dma((n,)), dma((outer,)), dma((outer,)), dma(()),
        ],
        compiler_params=pltpu.CompilerParams(
            collective_id=0, has_side_effects=True, vmem_limit_bytes=48 * 2**20
        ),
        name="tomography",
    )(rows, packed, filter_taps, conv2_weight, cotangent[0], *tables)
    grads = small[0].reshape(chans_dev, SLOTS)
    return (
        image[None],
        grads[:, 0:9].reshape(chans_dev, 3, 3),
        grads[:, 9],
        taps_out,
        grads[:, 16:25].reshape(chans_dev, 3, 3),
    )


def solution(mesh):
    sizes = tuple(mesh.shape[axis] for axis in ("ang", "row", "ch"))

    def whole(projections, conv1_weight, conv1_bias, filter_taps, conv2_weight, cotangent):
        tables = make_tables(projections.shape[-1])

        def local(*arrays):
            return on_device(sizes, tuple(jnp.asarray(t) for t in tables), *arrays)

        return jax.shard_map(
            local,
            mesh=mesh,
            in_specs=(
                P(("slab", "ang"), "row", None),
                P("ch", None, None),
                P("ch"),
                P("ch", None),
                P(),
                P(("slab", "row"), None, ("ang", "ch"), None),
            ),
            out_specs=(
                P(("slab", "row"), None, ("ang", "ch"), None),
                P(("slab", "ch"), None, None),
                P(("slab", "ch")),
                P(("slab", "ch"), None),
                P(("slab", "ch"), None, None),
            ),
            check_vma=False,
        )(projections, conv1_weight, conv1_bias, filter_taps, conv2_weight, cotangent)

    return whole
```

profile of v0, /device:TPU:0, one launch (start us, length us, event | category | flops | bytes accessed | tf_op | source)
XLA Modules:
  0.0 35.2 jit_solution(9915969346446367012)
XLA Ops:
  0.6 1.0 %pad.8 = f32[34,2048]{1,0:T(8,128)S(1)} pad(f32[32,2048]{1,0:T(8,128)} %bitcast.11, f32[]{:T(128)} %constant.6.clone.1), padding=1_1x0_0 | pad | bytes 540676 | tf_op jit(solution)/shard_map/jit(_pad)/pad | solution.py:467
  1.6 0.0 copy-start
  1.6 0.1 copy.23
  1.7 0.0 copy-start.5
  1.7 0.0 copy-start.4
  1.7 0.0 copy-start.1
  1.7 0.0 copy-start.2
  1.8 0.7 %copy-done.5 = f32[8,3,3]{0,2,1:T(4,128)S(1)} copy-done((f32[8,3,3]{0,2,1:T(4,128)S(1)}, f32[8,3,3]{0,2,1:T(4,128)}, u32[]{:S(2)}) %copy-start.5) | copy-done | bytes 312
  2.4 0.1 copy.20.second_ref
  2.5 0.0 copy-done.4
  2.5 0.1 reshape.23
  2.6 0.7 %copy-done.6 = f32[4]{0:T(128)S(1)} copy-done((f32[4]{0:T(128)S(1)}, f32[4]{0:T(128)}, u32[]{:S(2)}) %copy-start.6) | copy-done | bytes 40
  3.3 0.1 copy.19
  3.4 0.1 select_maximum_fusion.packed_ref
  3.5 28.2 %tomography.1 = (f32[4,4,2048]{2,1,0:T(4,128)S(1)}, f32[4,2048]{1,0:T(4,128)S(1)}, f32[8,128]{1,0:T(8,128)S(1)}) custom-call(f32[34,16,128]{2,1,0:T(8,128)S(1)} %slice.16.rows_ref, f32[4,128]{1,0:T(4,128)S(1)} %select_maximum_fusion.packed_ref, f32[4,2048]{1,0:T(4,128)S(1)} %copy-done.3, f32[8,3,3]{2,1,0:T(4,128)S(1)} %copy.20.second_ref, ...), custom_call_target="tpu_custom_call" | custom-call | tf_op jit(solution)/shard_map/tomography/pallas_call | solution.py:474
  31.7 0.1 reshape_squeeze.3
  31.8 0.1 fusion
  31.9 0.1 reshape.24
  32.0 0.6 %copy.21 = f32[4,3,3]{2,0,1:T(4,128)} copy(f32[4,3,3]{2,1,0:T(4,128)S(1)} %reshape.24) | data formatting | bytes 288
  32.6 0.1 reshape.25
  32.7 0.6 %copy.22 = f32[4,3,3]{2,0,1:T(4,128)} copy(f32[4,3,3]{2,1,0:T(4,128)S(1)} %reshape.25) | data formatting | bytes 288
  33.3 0.7 %slice_reduce_fusion = f32[4]{0:T(128)} fusion(f32[4,32]{1,0:T(4,128)S(1)} %reshape_squeeze.3), kind=kLoop, calls=%fused_computation.2 | loop fusion | bytes 32 | tf_op jit(solution)/shard_map/slice | solution.py:517
  34.0 0.7 %copy.26 = f32[1,4,4,2048]{3,2,1,0:T(4,128)} copy(f32[1,4,4,2048]{3,2,1,0:T(4,128)S(1)} %bitcast.8) | data formatting | bytes 262144
  34.6 0.6 %copy.27 = f32[4,2048]{1,0:T(4,128)} copy(f32[4,2048]{1,0:T(4,128)S(1)} %get-tuple-element.31) | data formatting | bytes 65536
  (9 shorter events, 0.1 us)
Async XLA Ops:
  1.6 1.8 %copy-start = (bf16[4,256,256]{2,1,0:T(8,128)(2,1)S(1)}, bf16[4,256,256]{2,1,0:T(8,128)(2,1)}, u32[]{:S(2)}) copy-start(bf16[4,256,256]{2,1,0:T(8,128)(2,1)} %constant.7.clone.tables_ref) | copy-start | bytes 1572868
  1.7 0.7 %copy-start.5 = (f32[8,3,3]{0,2,1:T(4,128)S(1)}, f32[8,3,3]{0,2,1:T(4,128)}, u32[]{:S(2)}) copy-start(f32[8,3,3]{0,2,1:T(4,128)} %param.12) | copy-start | bytes 868
  1.7 0.8 %copy-start.4 = (f32[4,3,3]{2,0,1:T(4,128)S(1)}, f32[4,3,3]{2,0,1:T(4,128)}, u32[]{:S(2)}) copy-start(f32[4,3,3]{2,0,1:T(4,128)} %param.9) | copy-start | bytes 436
  1.7 1.7 %copy-start.1 = (f32[1,4,4,2048]{3,2,1,0:T(4,128)S(1)}, f32[1,4,4,2048]{3,2,1,0:T(4,128)}, u32[]{:S(2)}) copy-start(f32[1,4,4,2048]{3,2,1,0:T(4,128)} %param.13) | copy-start | bytes 393220
  1.7 1.7 %copy-start.2 = (f32[2,128,128]{2,1,0:T(8,128)S(1)}, f32[2,128,128]{2,1,0:T(8,128)}, u32[]{:S(2)}) copy-start(f32[2,128,128]{2,1,0:T(8,128)} %constant.8.clone.turns_ref) | copy-start | bytes 393220
  2.4 1.0 %copy-start.3 = (f32[4,2048]{1,0:T(4,128)S(1)}, f32[4,2048]{1,0:T(4,128)}, u32[]{:S(2)}) copy-start(f32[4,2048]{1,0:T(4,128)} %taps_ref.1) | copy-start | bytes 98308
  2.6 0.7 %copy-start.6 = (f32[4]{0:T(128)S(1)}, f32[4]{0:T(128)}, u32[]{:S(2)}) copy-start(f32[4]{0:T(128)} %param.10) | copy-start | bytes 52
where the time goes:
time: 35.4 us; the launch traced here: 35.2 us
  Pallas kernels  28.2 us (80%)
  local copies, waits for them, and re-layouts  6.2 us (18%)
  between operations  0.72 us (2%)
    pallas_call x1, Pallas kernels, on_device(): pl.pallas_call(functools.partial(kernel, sizes), out_shape=(jax.ShapeDtyp...  28.2 us
    unnamed x21, local copies, waits for them, and re-layouts  3.99 us
    pad x1, local copies, waits for them, and re-layouts, on_device(): jnp.pad(projections[0], ((1, 1), (0, 0))).reshape(held + 2, outer, LANES)  0.98 us

commit v1 on v0

--- a/solution.py
+++ b/solution.py
@@ -79,21 +79,23 @@
 
 def kernel(
     sizes,
-    rows_ref, packed_ref, taps_ref, second_ref, cot_ref, tables_ref, turns_ref,
-    sino_ref, taps_out_ref, small_out_ref,
+    proj_hbm, first_hbm, bias_hbm, taps_hbm, second_ref, cot_hbm, tables_hbm, turns_hbm,
+    sino_ref, first_out_ref, bias_out_ref, taps_out_ref, second_out_ref,
+    proj_ref, first_vmem, bias_vmem, taps_ref, cot_ref, tables_ref, turns_ref,
+    rows_ref, packed_ref, small_in, small_own,
     got, top, bottom, all_taps, all_packed, first_ref,
     cot_shift, proj_shift, spec_back, spec_hidden, spec_taps, work,
     back, slope, filt, partial, mixed,
     outgoing, incoming, collected,
     rows_send, rows_recv, edge_send, edge_recv, taps_send, taps_recv,
-    packed_send, packed_recv, sum_send, sum_recv, gather_send, gather_recv, local_sem,
+    packed_send, packed_recv, sum_send, sum_recv, gather_send, gather_recv, small_send, small_recv, load_sem, local_sem,
 ):
     ang_n, row_n, ch_n = sizes
     n = ang_n * row_n * ch_n
     angles, rq, columns = cot_ref.shape
-    chans = second_ref.shape[0]
+    chans = second_ref.shape[2]
     chans_dev = taps_ref.shape[0]
-    held = rows_ref.shape[0] - 2
+    held = proj_ref.shape[0]
     both = angles * rq
     half = both // 2
     outer = columns // LANES
@@ -111,12 +113,40 @@
     def _(o):
         pl.semaphore_signal(barrier, inc=1, device_id=place((me + o) % n), device_id_type=MESH)
 
+    loads = [
+        pltpu.make_async_copy(source, target, load_sem.at[at])
+        for at, (source, target) in enumerate((
+            (proj_hbm, proj_ref), (first_hbm, first_vmem), (bias_hbm, bias_vmem),
+            (taps_hbm, taps_ref), (cot_hbm, cot_ref), (tables_hbm, tables_ref),
+            (turns_hbm, turns_ref)))
+    ]
+    for load in loads:
+        load.start()
+
+    def cols(m):
+        return slice(m * LANES, (m + 1) * LANES)
+
+    edge = jnp.zeros((outer, LANES), jnp.float32)
+    rows_ref[0:outer, :] = edge
+    rows_ref[(held + 1) * outer : (held + 2) * outer, :] = edge
+    packed_ref[...] = jnp.zeros(packed_ref.shape, jnp.float32)
+    loads[0].wait()
+    for at in range(0, held, 8):
+        for m in range(outer):
+            rows_ref[pl.ds((at + 1) * outer + m, 8, stride=outer), :] = proj_ref[at : at + 8, cols(m)]
+    loads[1].wait()
+    loads[2].wait()
+    for i in range(3):
+        packed_ref[:, 3 * i : 3 * i + 3] = first_vmem[i]
+    for l in range(chans_dev):
+        packed_ref[l : l + 1, 9:10] = bias_vmem[0:1, l : l + 1]
+    loads[3].wait()
     pl.semaphore_wait(barrier, n - 1)
 
     def rows_copy(o, slot, target):
-        start = (target * ch_n + c0) * rq
-        return pltpu.make_async_remote_copy(
-            src_ref=rows_ref.at[pl.ds(start, rq + 2)], dst_ref=got.at[slot],
+        start = pl.multiple_of((target * ch_n + c0) * rq * outer, outer)
+        return pltpu.make_async_remote_copy(
+            src_ref=rows_ref.at[pl.ds(start, (rq + 2) * outer)], dst_ref=got.at[slot],
             send_sem=rows_send.at[o], recv_sem=rows_recv.at[slot],
             device_id=(slab, target, k, c0), device_id_type=MESH)
 
@@ -134,13 +164,13 @@
 
     def top_copy(slot):
         return pltpu.make_async_remote_copy(
-            src_ref=rows_ref.at[held], dst_ref=top.at[slot],
+            src_ref=rows_ref.at[pl.ds(held * outer, outer)], dst_ref=top.at[slot],
             send_sem=edge_send.at[0], recv_sem=edge_recv.at[0, slot],
             device_id=(slab, 0, (k + 1) % row_n, 0), device_id_type=MESH)
 
     def bottom_copy(slot):
         return pltpu.make_async_remote_copy(
-            src_ref=rows_ref.at[1], dst_ref=bottom.at[slot],
+            src_ref=rows_ref.at[pl.ds(outer, outer)], dst_ref=bottom.at[slot],
             send_sem=edge_send.at[1], recv_sem=edge_recv.at[1, slot],
             device_id=(slab, ang_n - 1, (k + row_n - 1) % row_n, ch_n - 1), device_id_type=MESH)
 
@@ -161,7 +191,8 @@
     for o in range(1, ang_n):
         rows_copy(o, z, (z + o) % ang_n).start()
 
-    got[z] = rows_ref[pl.ds((z * ch_n + c0) * rq, rq + 2)]
+    mine_at = pl.multiple_of((z * ch_n + c0) * rq * outer, outer)
+    got[z] = rows_ref[pl.ds(mine_at, (rq + 2) * outer), :]
     all_taps[c0] = taps_ref[...]
     all_packed[c0] = packed_ref[...]
 
@@ -174,12 +205,10 @@
     def from_right(x):
         return jnp.where(last_col, 0.0, pltpu.roll(x, columns - 1, 1))
 
-    def cols(m):
-        return slice(m * LANES, (m + 1) * LANES)
-
     lo, hi = slice(0, half), slice(half, both)
     re_l, im_l = slice(0, LANES), slice(LANES, 2 * LANES)
 
+    loads[4].wait()
     upstream = jnp.concatenate([cot_ref[a] for a in range(angles)], axis=0)
     for i in range(3):
         shift = (i - 1) * rq % both
@@ -209,9 +238,12 @@
     def start_of(c):
         return pl.multiple_of(c * block, block)
 
+    loads[5].wait()
+    loads[6].wait()
+
     @pl.loop(0, chans)
     def _(c):
-        weights = [second_ref[c, t // 3, t % 3] for t in range(9)]
+        weights = [second_ref[t // 3, t % 3, c] for t in range(9)]
         values = []
         for m in range(outer):
             pair = []
@@ -270,22 +302,19 @@
     def _():
         for a in range(ang_n):
             top_copy(a).wait_recv()
-            got[a, 0] = top[a]
+            got[a, 0:outer, :] = top[a]
 
     @pl.when(jnp.logical_and(jnp.logical_and(z == ang_n - 1, c0 == ch_n - 1), k < row_n - 1))
     def _():
         for a in range(ang_n):
             bottom_copy(a).wait_recv()
-            got[a, rq + 1] = bottom[a]
+            got[a, (rq + 1) * outer : (rq + 2) * outer, :] = bottom[a]
 
     for a in range(angles):
-        for r in range(rq + 2):
-            line = got[a, r]
-            for i in range(3):
-                q = r - i
-                if 0 <= q < rq:
-                    for m in range(outer):
-                        proj_shift[3 * i + 1, a * rq + q : a * rq + q + 1, cols(m)] = line[m : m + 1, :]
+        for i in range(3):
+            for m in range(outer):
+                lines = got[a, pl.ds(i * outer + m, rq, stride=outer), :]
+                proj_shift[3 * i + 1, a * rq : (a + 1) * rq, cols(m)] = lines
     for i in range(3):
         centre = proj_shift[3 * i + 1]
         proj_shift[3 * i] = from_left(centre)
@@ -330,21 +359,22 @@
             work[at, re_l] = jnp.where(line_of == c, folded(gr * hr + gi * hi_), work[at, re_l])
             work[at, im_l] = jnp.where(line_of == c, folded(gr * hi_ - gi * hr), work[at, im_l])
 
-    for s in range(0, chans * block, step):
-        multiply(work, s, step, tables_ref, 2)
     multiply(work, chans * block, block, tables_ref, 2)
+    for m, (re, im) in enumerate(load_inverse(work, chans * block)):
+        outgoing[m] = re
+
+    def sum_copy(o, slot, target):
+        return pltpu.make_async_remote_copy(
+            src_ref=outgoing.at[target % outer], dst_ref=incoming.at[slot],
+            send_sem=sum_send.at[o], recv_sem=sum_recv.at[slot],
+            device_id=place(target), device_id_type=MESH)
+
+    @pl.loop(1, n)
+    def _(o):
+        sum_copy(o, me, (me + o) % n).start()
+
+    incoming[me] = outgoing[me % outer]
     partial[...] = jnp.zeros(partial.shape, jnp.float32)
-
-    @pl.loop(0, chans)
-    def _(c):
-        sums = [jnp.zeros((half, LANES), jnp.float32) for _ in range(9)]
-        for m, (re, im) in enumerate(load_inverse(work, start_of(c))):
-            filt[c, lo, cols(m)] = re
-            filt[c, hi, cols(m)] = im
-            for t in range(9):
-                sums[t] = sums[t] + re * cot_shift[t, lo, cols(m)] + im * cot_shift[t, hi, cols(m)]
-        for t in range(9):
-            partial[c, 16 + t : 17 + t, :] = folded(sums[t])
 
     @pl.loop(0, chans)
     def _(c):
@@ -358,26 +388,61 @@
         for t in range(10):
             partial[c, t : t + 1, :] = folded(sums[t])
 
+    for s in range(0, chans * block, step):
+        multiply(work, s, step, tables_ref, 2)
+
+    @pl.loop(0, chans)
+    def _(c):
+        sums = [jnp.zeros((half, LANES), jnp.float32) for _ in range(9)]
+        for m, (re, im) in enumerate(load_inverse(work, start_of(c))):
+            filt[c, lo, cols(m)] = re
+            filt[c, hi, cols(m)] = im
+            for t in range(9):
+                sums[t] = sums[t] + re * cot_shift[t, lo, cols(m)] + im * cot_shift[t, hi, cols(m)]
+        for t in range(9):
+            partial[c, 16 + t : 17 + t, :] = folded(sums[t])
+
     small = lax.dot_general(
-        jnp.ones((8, LANES), jnp.float32), partial[...].reshape(chans * SLOTS, LANES), (((1,), (1,)), ((), ())),
+        jnp.ones((8, LANES), jnp.float32), partial[...].reshape(chans * SLOTS, LANES),
+        (((1,), (1,)), ((), ())),
         precision=lax.Precision.HIGHEST, preferred_element_type=jnp.float32)
     width = chans_dev * SLOTS
-    for m, (re, im) in enumerate(load_inverse(work, chans * block)):
-        outgoing[m, 0:chans, :] = re
-        h = m % ch_n
-        outgoing[m, chans : chans + 1, :] = small[0:1, h * width : (h + 1) * width]
-
-    def sum_copy(o, slot, target):
-        return pltpu.make_async_remote_copy(
-            src_ref=outgoing.at[target % outer], dst_ref=incoming.at[slot],
-            send_sem=sum_send.at[o], recv_sem=sum_recv.at[slot],
+    for h in range(ch_n):
+        small_own[h] = small[0:1, h * width : (h + 1) * width]
+
+    def small_copy(o, slot, target):
+        return pltpu.make_async_remote_copy(
+            src_ref=small_own.at[target % ch_n], dst_ref=small_in.at[slot],
+            send_sem=small_send.at[o], recv_sem=small_recv.at[slot],
             device_id=place(target), device_id_type=MESH)
 
     @pl.loop(1, n)
     def _(o):
-        sum_copy(o, me, (me + o) % n).start()
-
-    incoming[me] = outgoing[me % outer]
+        small_copy(o, me, (me + o) % n).start()
+
+    small_in[me] = small_own[c0]
+
+    @pl.loop(1, n)
+    def _(o):
+        source = (me + o) % n
+        sum_copy(o, source, source).wait_recv()
+
+    total = incoming[0]
+    for d in range(1, n):
+        total = total + incoming[d]
+    mine = me % outer
+    group = me - mine
+    collected[mine] = total
+
+    def gather_copy(o, slot, target):
+        return pltpu.make_async_remote_copy(
+            src_ref=collected.at[mine], dst_ref=collected.at[slot],
+            send_sem=gather_send.at[o], recv_sem=gather_recv.at[slot],
+            device_id=place(group + target), device_id_type=MESH)
+
+    @pl.loop(1, outer)
+    def _(o):
+        gather_copy(o, mine, (mine + o) % outer).start()
 
     @pl.loop(0, outer)
     def _(m):
@@ -385,9 +450,9 @@
         for rows in (lo, hi):
             pieces = [filt[c, rows, at] for c in range(chans)]
             for t in range(9):
-                total = second_ref[0, t // 3, t % 3] * pieces[0]
+                total = second_ref[t // 3, t % 3, 0] * pieces[0]
                 for c in range(1, chans):
-                    total = total + second_ref[c, t // 3, t % 3] * pieces[c]
+                    total = total + second_ref[t // 3, t % 3, c] * pieces[c]
                 mixed[t, rows, at] = total
 
     sides = []
@@ -403,25 +468,17 @@
     @pl.loop(1, n)
     def _(o):
         source = (me + o) % n
-        sum_copy(o, source, source).wait_recv()
-
-    total = incoming[0]
+        small_copy(o, source, source).wait_recv()
+
+    sums = small_in[0]
     for d in range(1, n):
-        total = total + incoming[d]
-    small_out_ref[...] = jnp.broadcast_to(total[chans : chans + 1], small_out_ref.shape)
-    mine = me % outer
-    group = me - mine
-    collected[mine] = total[0:chans]
-
-    def gather_copy(o, slot, target):
-        return pltpu.make_async_remote_copy(
-            src_ref=collected.at[mine], dst_ref=collected.at[slot],
-            send_sem=gather_send.at[o], recv_sem=gather_recv.at[slot],
-            device_id=place(group + target), device_id_type=MESH)
-
-    @pl.loop(1, outer)
-    def _(o):
-        gather_copy(o, mine, (mine + o) % outer).start()
+        sums = sums + small_in[d]
+    for l in range(chans_dev):
+        for i in range(3):
+            at = l * SLOTS + 3 * i
+            first_out_ref[i, l : l + 1, :] = sums[:, at : at + 3]
+            second_out_ref[i, l : l + 1, :] = sums[:, at + 16 : at + 19]
+        bias_out_ref[0:1, l : l + 1] = sums[:, l * SLOTS + 9 : l * SLOTS + 10]
 
     @pl.loop(1, outer)
     def _(o):
@@ -448,10 +505,23 @@
     @pl.loop(1, n)
     def _(o):
         sum_copy(o, me, (me + o) % n).wait_send()
+        small_copy(o, me, (me + o) % n).wait_send()
 
     @pl.loop(1, outer)
     def _(o):
         gather_copy(o, mine, (mine + o) % outer).wait_send()
+
+
+def deliver(*refs):
+    count = len(refs) // 2
+    sems = refs[-1]
+    copies = [
+        pltpu.make_async_copy(refs[at], refs[count + at], sems.at[at]) for at in range(count)
+    ]
+    for copy in copies:
+        copy.start()
+    for copy in copies:
+        copy.wait()
 
 
 def on_device(sizes, tables, projections, conv1_weight, conv1_bias, filter_taps, conv2_weight, cotangent):
@@ -464,24 +534,36 @@
     outer = columns // LANES
     both = angles * rq
     block = outer * both // 2
-    rows = jnp.pad(projections[0], ((1, 1), (0, 0))).reshape(held + 2, outer, LANES)
-    packed = jnp.concatenate([conv1_weight.reshape(chans_dev, 9), conv1_bias[:, None]], axis=1)
-    packed = jnp.pad(packed, ((0, 0), (0, LANES - 10)))
     f32 = jnp.float32
     vmem = pl.BlockSpec(memory_space=pltpu.VMEM)
+    hbm = pl.BlockSpec(memory_space=pltpu.HBM)
     dma = pltpu.SemaphoreType.DMA
     wide = (both, columns)
-    image, taps_out, small = pl.pallas_call(
+    shapes = (
+        jax.ShapeDtypeStruct((angles, rq, columns), f32),
+        jax.ShapeDtypeStruct((3, chans_dev, 3), f32),
+        jax.ShapeDtypeStruct((1, chans_dev), f32),
+        jax.ShapeDtypeStruct((chans_dev, columns), f32),
+        jax.ShapeDtypeStruct((3, chans_dev, 3), f32),
+    )
+    results = pl.pallas_call(
         functools.partial(kernel, sizes),
-        out_shape=(
-            jax.ShapeDtypeStruct((angles, rq, columns), f32),
-            jax.ShapeDtypeStruct((chans_dev, columns), f32),
-            jax.ShapeDtypeStruct((8, LANES), f32),
-        ),
-        in_specs=[vmem, vmem, vmem, pl.BlockSpec(memory_space=pltpu.SMEM), vmem, vmem, vmem],
-        out_specs=(vmem, vmem, vmem),
+        out_shape=shapes,
+        in_specs=[hbm] * 4 + [pl.BlockSpec(memory_space=pltpu.SMEM)] + [hbm] * 3,
+        out_specs=(vmem,) * 5,
         scratch_shapes=[
-            pltpu.VMEM((ang_n, rq + 2, outer, LANES), f32),
+            pltpu.VMEM((held, columns), f32),
+            pltpu.VMEM((3, chans_dev, 3), f32),
+            pltpu.VMEM((1, chans_dev), f32),
+            pltpu.VMEM((chans_dev, columns), f32),
+            pltpu.VMEM((angles, rq, columns), f32),
+            pltpu.VMEM(tables[0].shape, jnp.bfloat16),
+            pltpu.VMEM(tables[1].shape, f32),
+            pltpu.VMEM(((held + 2) * outer, LANES), f32),
+            pltpu.VMEM((chans_dev, LANES), f32),
+            pltpu.VMEM((n, 1, LANES), f32),
+            pltpu.VMEM((ch_n, 1, LANES), f32),
+            pltpu.VMEM((ang_n, (rq + 2) * outer, LANES), f32),
             pltpu.VMEM((ang_n, outer, LANES), f32),
             pltpu.VMEM((ang_n, outer, LANES), f32),
             pltpu.VMEM((ch_n, chans_dev, columns), f32),
@@ -498,25 +580,34 @@
             pltpu.VMEM((chans,) + wide, f32),
             pltpu.VMEM((chans, SLOTS, LANES), f32),
             pltpu.VMEM((9,) + wide, f32),
-            pltpu.VMEM((outer, chans + 1, LANES), f32),
-            pltpu.VMEM((n, chans + 1, LANES), f32),
+            pltpu.VMEM((outer, chans, LANES), f32),
+            pltpu.VMEM((n, chans, LANES), f32),
             pltpu.VMEM((outer, chans, LANES), f32),
             dma((ang_n,)), dma((ang_n,)), dma((2,)), dma((2, ang_n)),
             dma((ch_n,)), dma((ch_n,)), dma((ch_n,)), dma((ch_n,)),
-            dma((n,)), dma((n,)), dma((outer,)), dma((outer,)), dma(()),
+            dma((n,)), dma((n,)), dma((outer,)), dma((outer,)),
+            dma((n,)), dma((n,)), dma((7,)), dma(()),
         ],
         compiler_params=pltpu.CompilerParams(
-            collective_id=0, has_side_effects=True, vmem_limit_bytes=48 * 2**20
+            collective_id=0, has_side_effects=True, vmem_limit_bytes=63 * 2**20
         ),
         name="tomography",
-    )(rows, packed, filter_taps, conv2_weight, cotangent[0], *tables)
-    grads = small[0].reshape(chans_dev, SLOTS)
+    )(
+        projections[0], jnp.transpose(conv1_weight, (1, 0, 2)), conv1_bias[None], filter_taps,
+        jnp.transpose(conv2_weight, (1, 2, 0)), cotangent[0], *tables,
+    )
+    image, first, bias, taps_out, second = pl.pallas_call(
+        deliver,
+        out_shape=shapes,
+        in_specs=[hbm] * 5,
+        out_specs=(hbm,) * 5,
+        scratch_shapes=[dma((5,))],
+        compiler_params=pltpu.CompilerParams(vmem_limit_bytes=63 * 2**20),
+        name="deliver",
+    )(*results)
     return (
-        image[None],
-        grads[:, 0:9].reshape(chans_dev, 3, 3),
-        grads[:, 9],
-        taps_out,
-        grads[:, 16:25].reshape(chans_dev, 3, 3),
+        image[None], jnp.transpose(first, (1, 0, 2)), bias[0], taps_out,
+        jnp.transpose(second, (1, 0, 2)),
     )
 
 

time: 35.4 us -> 33.8 us (0.955)
  local copies, waits for them, and re-layouts: 6.2 us -> 0 us
  Pallas kernels: 28.2 us -> 33 us
    pallas_call x1 -> x2, Pallas kernels: 28.2 us -> 33 us  [the longest x1 26.5 us: on_device(): pl.pallas_call(functools.partial(kernel, sizes), out_shape=shapes, in_spe...]
    unnamed x21 -> x0, local copies, waits for them, and re-layouts: 3.99 us -> none
    pad x1 -> x0, local copies, waits for them, and re-layouts: 0.98 us -> none  [on_device(): jnp.pad(projections[0], ((1, 1), (0, 0))).reshape(held + 2, outer, LANES)]
    slice x3 -> x0, local copies, waits for them, and re-layouts: 0.79 us -> none  [the longest x1 0.69 us: on_device(): grads[:, 9]]
where the time goes in v1:
time: 33.8 us; the launch traced here: 33.6 us
  Pallas kernels  33 us (98%)
  between operations  0.64 us (2%)
    pallas_call x1, Pallas kernels, on_device(): pl.pallas_call(functools.partial(kernel, sizes), out_shape=shapes, in_spe...  26.5 us
    pallas_call x1, Pallas kernels, on_device(): pl.pallas_call(deliver, out_shape=shapes, in_specs=[hbm] * 5, out_specs=(...  6.5 us

profile of v1, /device:TPU:0, one launch (start us, length us, event | category | flops | bytes accessed | tf_op | source)
XLA Modules:
  0.0 33.6 jit_solution(418442731777164016)
XLA Ops:
  0.6 26.5 %tomography.1 = (f32[4,4,2048]{2,1,0:T(4,128)}, f32[3,4,3]{2,1,0:T(4,128)}, f32[1,4]{1,0:T(1,128)}, f32[4,2048]{1,0:T(4,128)}, f32[3,4,3]{2,1,0:T(4,128)}) custom-call(f32[32,2048]{1,0:T(8,128)} %bitcast.9, f32[3,4,3]{2,1,0:T(4,128)} %bitcast.11, f32[1,4]{1,0:T(1,128)} %bitcast.13, f32[4,2048]{1,0:T(4,128)} %taps_hbm.1, f32[3,3,8]{2,1,0:T(4,128)} %bitcast.12, ...), custom_call_target="tpu_custom_call" | custom-call | tf_op jit(solution)/shard_map/tomography/pallas_call | solution.py:549
  27.1 6.5 %deliver.1 = (f32[4,4,2048]{2,1,0:T(4,128)}, f32[3,4,3]{2,1,0:T(4,128)}, f32[1,4]{1,0:T(1,128)}, f32[4,2048]{1,0:T(4,128)}, f32[3,4,3]{2,1,0:T(4,128)}) custom-call(f32[4,4,2048]{2,1,0:T(4,128)} %get-tuple-element.15.refs_0_, f32[3,4,3]{2,1,0:T(4,128)} %get-tuple-element.16.refs_1_, f32[1,4]{1,0:T(1,128)} %get-tuple-element.17.refs_2_, ...), custom_call_target="tpu_custom_call" | custom-call | tf_op jit(solution)/shard_map/deliver/pallas_call | solution.py:599

commit v2 on v1

--- a/solution.py
+++ b/solution.py
@@ -513,14 +513,17 @@
 
 
 def deliver(*refs):
-    count = len(refs) // 2
+    count = (len(refs) - 1) // 3
+    sources, targets, staged = refs[:count], refs[count : 2 * count], refs[2 * count : 3 * count]
     sems = refs[-1]
-    copies = [
-        pltpu.make_async_copy(refs[at], refs[count + at], sems.at[at]) for at in range(count)
-    ]
-    for copy in copies:
+    into = [pltpu.make_async_copy(sources[at], staged[at], sems.at[0, at]) for at in range(count)]
+    out = [pltpu.make_async_copy(staged[at], targets[at], sems.at[1, at]) for at in range(count)]
+    for copy in into:
         copy.start()
-    for copy in copies:
+    for copy_in, copy_out in zip(into, out):
+        copy_in.wait()
+        copy_out.start()
+    for copy in out:
         copy.wait()
 
 
@@ -601,7 +604,7 @@
         out_shape=shapes,
         in_specs=[hbm] * 5,
         out_specs=(hbm,) * 5,
-        scratch_shapes=[dma((5,))],
+        scratch_shapes=[pltpu.VMEM(leaf.shape, f32) for leaf in shapes] + [dma((2, 5))],
         compiler_params=pltpu.CompilerParams(vmem_limit_bytes=63 * 2**20),
         name="deliver",
     )(*results)

time: 33.8 us -> 29 us (0.86)
  Pallas kernels: 33 us -> 28.1 us
    pallas_call x1, Pallas kernels: 6.5 us -> 1.66 us  [on_device(): pl.pallas_call(deliver, out_shape=shapes, in_specs=[hbm] * 5, out_specs=(...]
where the time goes in v2:
time: 29 us; the launch traced here: 28.8 us
  Pallas kernels  28.1 us (97%)
  between operations  0.64 us (2%)
    pallas_call x1, Pallas kernels, on_device(): pl.pallas_call(functools.partial(kernel, sizes), out_shape=shapes, in_spe...  26.5 us
    pallas_call x1, Pallas kernels, on_device(): pl.pallas_call(deliver, out_shape=shapes, in_specs=[hbm] * 5, out_specs=(...  1.66 us

profile of v2, /device:TPU:0, one launch (start us, length us, event | category | flops | bytes accessed | tf_op | source)
XLA Modules:
  0.0 28.8 jit_solution(10680871246932378235)
XLA Ops:
  0.6 26.5 %tomography.1 = (f32[4,4,2048]{2,1,0:T(4,128)}, f32[3,4,3]{2,1,0:T(4,128)}, f32[1,4]{1,0:T(1,128)}, f32[4,2048]{1,0:T(4,128)}, f32[3,4,3]{2,1,0:T(4,128)}) custom-call(f32[32,2048]{1,0:T(8,128)} %bitcast.9, f32[3,4,3]{2,1,0:T(4,128)} %bitcast.11, f32[1,4]{1,0:T(1,128)} %bitcast.13, f32[4,2048]{1,0:T(4,128)} %taps_hbm.1, f32[3,3,8]{2,1,0:T(4,128)} %bitcast.12, ...), custom_call_target="tpu_custom_call" | custom-call | tf_op jit(solution)/shard_map/tomography/pallas_call | solution.py:552
  27.1 1.7 %deliver.1 = (f32[4,4,2048]{2,1,0:T(4,128)}, f32[3,4,3]{2,1,0:T(4,128)}, f32[1,4]{1,0:T(1,128)}, f32[4,2048]{1,0:T(4,128)}, f32[3,4,3]{2,1,0:T(4,128)}) custom-call(f32[4,4,2048]{2,1,0:T(4,128)} %get-tuple-element.15.refs_0_, f32[3,4,3]{2,1,0:T(4,128)} %get-tuple-element.16.refs_1_, f32[1,4]{1,0:T(1,128)} %get-tuple-element.17.refs_2_, ...), custom_call_target="tpu_custom_call" | custom-call | tf_op jit(solution)/shard_map/deliver/pallas_call | solution.py:602

commit v3 on v2

--- a/solution.py
+++ b/solution.py
@@ -174,6 +174,9 @@
             send_sem=edge_send.at[1], recv_sem=edge_recv.at[1, slot],
             device_id=(slab, ang_n - 1, (k + row_n - 1) % row_n, ch_n - 1), device_id_type=MESH)
 
+    for o in range(1, ang_n):
+        rows_copy(o, z, (z + o) % ang_n).start()
+
     for o in range(1, ch_n):
         taps_copy(o, c0, (c0 + o) % ch_n).start()
         packed_copy(o, c0, (c0 + o) % ch_n).start()
@@ -187,9 +190,6 @@
     @pl.when(sends_bottom)
     def _():
         bottom_copy(z).start()
-
-    for o in range(1, ang_n):
-        rows_copy(o, z, (z + o) % ang_n).start()
 
     mine_at = pl.multiple_of((z * ch_n + c0) * rq * outer, outer)
     got[z] = rows_ref[pl.ds(mine_at, (rq + 2) * outer), :]

time: 29 us -> 29.4 us (1.014)
  Pallas kernels: 28.1 us -> 28.6 us
    pallas_call x1, Pallas kernels: 26.5 us -> 26.9 us  [on_device(): pl.pallas_call(functools.partial(kernel, sizes), out_shape=shapes, in_spe...]
where the time goes in v3:
time: 29.4 us; the launch traced here: 29.2 us
  Pallas kernels  28.6 us (97%)
  between operations  0.64 us (2%)
    pallas_call x1, Pallas kernels, on_device(): pl.pallas_call(functools.partial(kernel, sizes), out_shape=shapes, in_spe...  26.9 us
    pallas_call x1, Pallas kernels, on_device(): pl.pallas_call(deliver, out_shape=shapes, in_specs=[hbm] * 5, out_specs=(...  1.66 us

profile of v3, /device:TPU:0, one launch (start us, length us, event | category | flops | bytes accessed | tf_op | source)
XLA Modules:
  0.0 29.2 jit_solution(8049136261765415461)
XLA Ops:
  0.6 26.9 %tomography.1 = (f32[4,4,2048]{2,1,0:T(4,128)}, f32[3,4,3]{2,1,0:T(4,128)}, f32[1,4]{1,0:T(1,128)}, f32[4,2048]{1,0:T(4,128)}, f32[3,4,3]{2,1,0:T(4,128)}) custom-call(f32[32,2048]{1,0:T(8,128)} %bitcast.9, f32[3,4,3]{2,1,0:T(4,128)} %bitcast.11, f32[1,4]{1,0:T(1,128)} %bitcast.13, f32[4,2048]{1,0:T(4,128)} %taps_hbm.1, f32[3,3,8]{2,1,0:T(4,128)} %bitcast.12, ...), custom_call_target="tpu_custom_call" | custom-call | tf_op jit(solution)/shard_map/tomography/pallas_call | solution.py:552
  27.6 1.7 %deliver.1 = (f32[4,4,2048]{2,1,0:T(4,128)}, f32[3,4,3]{2,1,0:T(4,128)}, f32[1,4]{1,0:T(1,128)}, f32[4,2048]{1,0:T(4,128)}, f32[3,4,3]{2,1,0:T(4,128)}) custom-call(f32[4,4,2048]{2,1,0:T(4,128)} %get-tuple-element.15.refs_0_, f32[3,4,3]{2,1,0:T(4,128)} %get-tuple-element.16.refs_1_, f32[1,4]{1,0:T(1,128)} %get-tuple-element.17.refs_2_, ...), custom_call_target="tpu_custom_call" | custom-call | tf_op jit(solution)/shard_map/deliver/pallas_call | solution.py:602
